TPU v7x, 32 devices: a whole 2x2x4 slice. The times are simulated.
32 devices in a mesh: ty: 4 (over y, x), tx: 8 (over z, core).
Axes of the slice: x: 2, y: 2, z: 4, core: 2. Of those that a mesh axis runs over, the one named last changes fastest.
Arguments:
- channel_cube: bfloat16 [256, 512, 128], P(('ty', 'tx'))
- footprint: int32 [32, 8], replicated, may hold values 0 or 1
- kernel_sigmas: int32 [4], replicated, may hold values from 1 to 3, as said below
- spectral_taps: int32 [2, 4], replicated, may hold values from 1 to 5, as said below
Outputs:
- snr_cubes: bfloat16 [4, 512, 128, 256], P(None, 'ty', 'tx')
Inputs may be any that keep to these rules, and one draw needn't show every extreme that they name: `kernel_sigmas`: some scale has exactly 3. `spectral_taps`: row 0 holds widths up to 5, row 1 dilations up to 4; some scale has width 5 and dilation 4 together.
All inputs are finite; a program needn't handle non-finite values.
Results may differ from a plain program's by a relative error of at most 0.0077.
Values may be sent and summed in bfloat16 or wider, within the bound.
No kernel may reach another device: no remote copies, remote signals or barrier semaphores. Data moves between devices by JAX's collectives and lax.ppermute only.
A program may use at most 192 MiB of HBM per device.

v0:
```python
import jax
import jax.numpy as jnp
from jax import lax
from jax.sharding import PartitionSpec as P

TILE_Y = 128
TILE_X = 16
NSC = 4
WMAX = 5
PT = 16
HALO = 9
PADC = 8


def with_halo(x, sides, width):
    for axis, dim in sides:
        peers, length = (lax.axis_size(axis), x.shape[dim])
        up = [(i, (i + 1) % peers) for i in range(peers - 1)]
        down = [(j, i) for i, j in up]
        last = lax.slice_in_dim(x, length - width, length, axis=dim)
        leading = lax.slice_in_dim(x, 0, width, axis=dim)
        before = lax.ppermute(last, axis, up)
        after = lax.ppermute(leading, axis, down)
        x = jnp.concatenate([before, x, after], axis=dim)
    return x


def gauss_taps(sigma_value):
    offsets = jnp.arange(-HALO, HALO + 1).astype(jnp.float32)
    spread = sigma_value.astype(jnp.float32)
    weights = jnp.exp(-offsets * offsets / (2.0 * spread * spread))
    weights = jnp.where(jnp.abs(offsets) <= 3.0 * spread, weights, jnp.float32(0.0))
    return weights / jnp.sum(weights)


def boxcar(field, width, dilation):
    last = field.ndim - 1
    channels = field.shape[last]
    pads = [(0, 0)] * last + [(PADC, PADC)]
    padded = jnp.pad(field, pads)
    total = jnp.zeros(field.shape, jnp.float32)
    for step in range(WMAX):
        start = PADC + dilation * (step - (width - 1) // 2)
        piece = lax.dynamic_slice_in_dim(padded, start, channels, last)
        total = total + jnp.where(step < width, piece, jnp.float32(0.0))
    return total / width.astype(jnp.float32)


def band_matrix(taps_bf, length):
    out_index = jnp.arange(length)[:, None, None]
    in_index = jnp.arange(length + 2 * HALO)[None, :, None]
    tap_index = jnp.arange(2 * HALO + 1)[None, None, :]
    chosen = jnp.where(
        in_index - out_index == tap_index,
        taps_bf.astype(jnp.float32)[None, None, :],
        jnp.float32(0.0),
    )
    return jnp.sum(chosen, axis=2).astype(jnp.bfloat16)


def relay(pieces):
    ch_local, n_rows, n_cols, cells = pieces.shape
    arrived = lax.all_to_all(
        pieces.reshape(ch_local, n_rows * n_cols, cells),
        ("ty", "tx"),
        split_axis=1,
        concat_axis=0,
        tiled=True,
    )
    return arrived.reshape(-1, cells)


def local(channel_cube, footprint, kernel_sigmas, spectral_taps):
    n_rows = lax.axis_size("ty")
    n_cols = lax.axis_size("tx")
    ch_local, full_y, full_x = channel_cube.shape
    pixel_mask = jnp.repeat(jnp.repeat(footprint, PT, 0), PT, 1).astype(jnp.float32)
    count = jnp.maximum(jnp.sum(pixel_mask), jnp.float32(1.0))
    row_start = lax.axis_index("ty") * TILE_Y
    col_start = lax.axis_index("tx") * TILE_X
    tile_mask = lax.dynamic_slice(pixel_mask, (row_start, col_start), (TILE_Y, TILE_X))
    plane_vals = jnp.where(
        pixel_mask[None] > 0.5, channel_cube.astype(jnp.float32), jnp.float32(0.0)
    )
    local_squares = jnp.sum(plane_vals * plane_vals, axis=(1, 2))
    squares = lax.all_gather(local_squares, ("ty", "tx"), axis=0, tiled=True)
    pieces = channel_cube.reshape(ch_local, n_rows, TILE_Y, n_cols, TILE_X).transpose(0, 1, 3, 2, 4)
    arrived = relay(pieces.reshape(ch_local, n_rows, n_cols, TILE_Y * TILE_X))
    channels = arrived.shape[0]
    tile_cells = arrived.T.reshape(TILE_Y, TILE_X, channels)
    tile_cells = jnp.where(tile_mask[:, :, None] > 0.5, tile_cells, jnp.zeros_like(tile_cells))
    padded = with_halo(tile_cells, (("ty", 0), ("tx", 1)), HALO)
    channel_noise = jnp.sqrt(squares / count + 1e-06)
    results = []
    for scale_idx in range(NSC):
        taps = gauss_taps(kernel_sigmas[scale_idx])
        taps_bf = taps.astype(jnp.bfloat16)
        row_band = band_matrix(taps_bf, TILE_Y)
        col_band = band_matrix(taps_bf, TILE_X)
        rows_pass = jnp.einsum(
            "ij,jxc->ixc", row_band, padded, preferred_element_type=jnp.float32
        ).astype(jnp.bfloat16)
        smooth = jnp.einsum("xk,ykc->yxc", col_band, rows_pass, preferred_element_type=jnp.float32)
        width = spectral_taps[0, scale_idx]
        dilation = spectral_taps[1, scale_idx]
        boxed = boxcar(smooth, width, dilation)
        knorm = jnp.sum(taps * taps) / jnp.sqrt(width.astype(jnp.float32))
        scaled = boxed * tile_mask[:, :, None] / (channel_noise[None, None, :] * knorm)
        results.append(scaled.astype(jnp.bfloat16))
    return jnp.stack(results)


def solution(mesh):
    placed = (P(("ty", "tx"), None, None), P(), P(), P())
    return jax.shard_map(
        local, mesh=mesh, in_specs=placed, out_specs=P(None, "ty", "tx", None), check_vma=False
    )
```

profile of v0, /device:TPU:3, one launch (start us, length us, event | category | flops | bytes accessed | tf_op | source)
XLA Modules:
  0.0 176.3 jit_solution(6123437555780068440)
XLA Ops:
  0.0 1.5 copy.34
  1.8 5.8 %copy.45 = bf16[8,4,8,128,16]{4,3,0,2,1:T(8,128)(2,1)} copy(bf16[8,4,8,128,16]{3,1,4,2,0:T(4,128)(2,1)S(1)} %bitcast.95) | data formatting | bytes 2097152 | tf_op jit(solution)/shard_map/reshape;reshape | solution.py:64
  7.5 15.8 %reshape.174 = bf16[8,32,2048]{2,0,1:T(8,128)(2,1)} reshape(bf16[8,4,8,128,16]{4,3,0,2,1:T(8,128)(2,1)} %copy.45) | data formatting | bytes 2097152 | tf_op jit(solution)/shard_map/reshape;reshape | solution.py:64
  23.4 6.4 %all-to-all-start = ((bf16[8,32,2048]{2,0,1:T(8,128)(2,1)}), bf16[8,32,2048]{2,0,1:T(8,128)(2,1)S(1)}, u32[]{:S(2)}, u32[]{:S(2)}) async-start(bf16[8,32,2048]{2,0,1:T(8,128)(2,1)} %reshape.174), calls=%async_computation | async-start | bytes 2097152 | tf_op jit(solution)/shard_map/all_to_all | solution.py:63
  65.7 1.3 multiply_reduce_fusion.4
  69.6 1.2 multiply_reduce_fusion.3
  72.1 1.3 multiply_reduce_fusion.2
  74.7 1.4 multiply_reduce_fusion.1
  77.5 38.9 %all-reduce.4 = f32[256]{0:T(256)S(1)} all-reduce(f32[256]{0:T(256)S(1)} %dynamic-update-slice), channel_id=1, replica_groups=mesh['ty'=4,'tx'=8] {'ty','tx'}, use_global_device_ids=true, to_apply=%add.4 | all-reduce | flops 256 | bytes 2048
  116.4 1.3 convert_convert_fusion
  117.7 1.3 convert_convert_fusion.2
  120.5 3.1 %collective-permute-start = (bf16[9,16,256]{2,0,1:T(8,128)(2,1)S(1)}, bf16[9,16,256]{2,0,1:T(8,128)(2,1)S(1)}, u32[]{:S(2)}, u32[]{:S(2)}) collective-permute-start(bf16[9,16,256]{2,0,1:T(8,128)(2,1)S(1)} %get-tuple-element.19), channel_id=1, source_target_pairs={{0,8},{8,16},{16,24},{1,9},{9,17},{17,25},{2,10},{10,18},{18,26},{... | collective-permute-start | bytes 221192 | tf_op jit(solution)/shard_map/ppermute | solution.py:22
  123.6 2.2 %collective-permute-start.1 = (bf16[9,16,256]{2,0,1:T(8,128)(2,1)S(1)}, bf16[9,16,256]{2,0,1:T(8,128)(2,1)S(1)}, u32[]{:S(2)}, u32[]{:S(2)}) collective-permute-start(bf16[9,16,256]{2,0,1:T(8,128)(2,1)S(1)} %get-tuple-element.20), channel_id=1, source_target_pairs={{8,0},{16,8},{24,16},{9,1},{17,9},{25,17},{10,2},{18,10},{26,18},{... | collective-permute-start | bytes 221192 | tf_op jit(solution)/shard_map/ppermute | solution.py:23
  126.2 4.3 %collective-permute-done.1 = bf16[9,16,256]{2,0,1:T(8,128)(2,1)S(1)} collective-permute-done((bf16[9,16,256]{2,0,1:T(8,128)(2,1)S(1)}, bf16[9,16,256]{2,0,1:T(8,128)(2,1)S(1)}, u32[]{:S(2)}, u32[]{:S(2)}) %collective-permute-start.1) | collective-permute-done | bytes 73760 | tf_op jit(solution)/shard_map/ppermute | solution.py:23
  131.0 6.6 %collective-permute-start.2 = (bf16[146,9,256]{2,0,1:T(8,128)(2,1)S(1)}, bf16[146,9,256]{2,0,1:T(8,128)(2,1)S(1)}, u32[]{:S(2)}, u32[]{:S(2)}) collective-permute-start(bf16[146,9,256]{2,0,1:T(8,128)(2,1)S(1)} %get-tuple-element.17), channel_id=1, source_target_pairs={{0,1},{1,2},{2,3},{3,4},{4,5},{5,6},{6,7},{8,9},{9,10},{10,11},{11... | collective-permute-start | bytes 2018312 | tf_op jit(solution)/shard_map/ppermute | solution.py:22
  137.6 2.1 %collective-permute-start.3 = (bf16[146,9,256]{2,0,1:T(8,128)(2,1)S(1)}, bf16[146,9,256]{2,0,1:T(8,128)(2,1)S(1)}, u32[]{:S(2)}, u32[]{:S(2)}) collective-permute-start(bf16[146,9,256]{2,0,1:T(8,128)(2,1)S(1)} %get-tuple-element.18), channel_id=1, source_target_pairs={{1,0},{2,1},{3,2},{4,3},{5,4},{6,5},{7,6},{9,8},{10,9},{11,10},{12... | collective-permute-start | bytes 2018312 | tf_op jit(solution)/shard_map/ppermute | solution.py:23
  139.8 0.8 select_reduce_fusion.3
  140.6 5.0 %collective-permute-done.2 = bf16[146,9,256]{2,0,1:T(8,128)(2,1)S(1)} collective-permute-done((bf16[146,9,256]{2,0,1:T(8,128)(2,1)S(1)}, bf16[146,9,256]{2,0,1:T(8,128)(2,1)S(1)}, u32[]{:S(2)}, u32[]{:S(2)}) %collective-permute-start.2) | collective-permute-done | bytes 672800 | tf_op jit(solution)/shard_map/ppermute | solution.py:22
  145.6 4.4 %collective-permute-done.3 = bf16[146,9,256]{2,0,1:T(8,128)(2,1)S(1)} collective-permute-done((bf16[146,9,256]{2,0,1:T(8,128)(2,1)S(1)}, bf16[146,9,256]{2,0,1:T(8,128)(2,1)S(1)}, u32[]{:S(2)}, u32[]{:S(2)}) %collective-permute-start.3) | collective-permute-done | bytes 672800 | tf_op jit(solution)/shard_map/ppermute | solution.py:23
  150.0 1.2 convolution_convert_fusion.3
  151.3 1.3 fusion.48
  152.6 1.2 convolution_convert_fusion.2
  153.9 1.3 fusion.51
  155.2 1.2 convolution_convert_fusion.1
  156.5 1.3 fusion.54
  157.8 1.2 convolution_convert_fusion
  159.0 1.3 fusion.57
  160.4 3.2 %fusion.60 = bf16[1,128,16,256]{3,2,1,0:T(8,128)(2,1)S(1)} fusion(f32[256]{0:T(256)S(1)} %get-tuple-element.13, f32[128,16]{1,0:T(8,128)S(1)} %copy.40, f32[]{:T(128)} %bitcast.18, s32[]{:T(128)S(6)} %select_n.301, f32[128,16,256]{2,1,0:T(8,128)S(1)} %fusion.48, pred[]{:T(512)} %bitcast.17, s32[]{:T(128)S(6)} %select_n.298, pred[]{:T(512)} %bitcast.16, ...), kind=kLoop, calls=%fused_computation.90 | loop fusion | flops 6815744 | bytes 3154973 | tf_op jit(solution)/shard_map/stack | solution.py:110
  163.6 3.4 %fusion.61 = bf16[1,128,16,256]{3,2,1,0:T(8,128)(2,1)S(1)} fusion(f32[256]{0:T(256)S(1)} %get-tuple-element.29, f32[128,16]{1,0:T(8,128)S(1)} %copy.40, f32[]{:T(128)} %bitcast.31, s32[]{:T(128)S(6)} %select_n.321, f32[128,16,256]{2,1,0:T(8,128)S(1)} %fusion.51, pred[]{:T(512)} %bitcast.30, s32[]{:T(128)S(6)} %select_n.318, pred[]{:T(512)} %bitcast.29, ...), kind=kLoop, calls=%fused_computation.91 | loop fusion | flops 6815744 | bytes 3154973 | tf_op jit(solution)/shard_map/stack | solution.py:110
  167.0 3.6 %fusion.62 = bf16[1,128,16,256]{3,2,1,0:T(8,128)(2,1)S(1)} fusion(f32[256]{0:T(256)S(1)} %get-tuple-element.30, f32[128,16]{1,0:T(8,128)S(1)} %copy.40, f32[]{:T(128)} %bitcast.44, s32[]{:T(128)S(6)} %select_n.340, f32[128,16,256]{2,1,0:T(8,128)S(1)} %fusion.54, pred[]{:T(512)} %bitcast.43, s32[]{:T(128)S(6)} %select_n.337, pred[]{:T(512)} %bitcast.42, ...), kind=kLoop, calls=%fused_computation.92 | loop fusion | flops 6815744 | bytes 3154973 | tf_op jit(solution)/shard_map/stack | solution.py:110
  170.6 3.4 %fusion.63 = bf16[1,128,16,256]{3,2,1,0:T(8,128)(2,1)S(1)} fusion(f32[256]{0:T(256)S(1)} %get-tuple-element.31, f32[128,16]{1,0:T(8,128)S(1)} %copy.40, f32[]{:T(128)} %bitcast.57, s32[]{:T(128)S(6)} %select_n.359, f32[128,16,256]{2,1,0:T(8,128)S(1)} %fusion.57, pred[]{:T(512)} %bitcast.56, s32[]{:T(128)S(6)} %select_n.356, pred[]{:T(512)} %bitcast.55, ...), kind=kLoop, calls=%fused_computation.93 | loop fusion | flops 6815744 | bytes 3154973 | tf_op jit(solution)/shard_map/stack | solution.py:110
  174.0 2.3 %pad_maximum_fusion = bf16[4,128,16,256]{3,2,1,0:T(8,128)(2,1)} fusion(bf16[1,128,16,256]{3,2,1,0:T(8,128)(2,1)S(1)} %fusion.63, bf16[1,128,16,256]{3,2,1,0:T(8,128)(2,1)S(1)} %fusion.62, bf16[1,128,16,256]{3,2,1,0:T(8,128)(2,1)S(1)} %fusion.61, bf16[1,128,16,256]{3,2,1,0:T(8,128)(2,1)S(1)} %fusion.60), kind=kLoop, calls=%fused_computation.20 | loop fusion | flops 6291456 | bytes 8388608 | tf_op jit(solution)/shard_map/stack | solution.py:110
  (39 shorter events, 8.6 us)
Async XLA Ops:
  23.3 6.4 %copy-start.2 = (s32[4]{0:T(128)S(1)}, s32[4]{0:T(128)}, u32[]{:S(2)}) copy-start(s32[4]{0:T(128)} %param.6) | copy-start | bytes 52
  23.3 9.8 %copy-start.1 = (s32[2,4]{1,0:T(2,128)S(1)}, s32[2,4]{1,0:T(2,128)}, u32[]{:S(2)}) copy-start(s32[2,4]{1,0:T(2,128)} %param.7) | copy-start | bytes 100
  23.3 40.8 %copy-start.3 = (s32[32,8]{0,1:T(8,128)S(1)}, s32[32,8]{0,1:T(8,128)}, u32[]{:S(2)}) copy-start(s32[32,8]{0,1:T(8,128)} %param.5) | copy-start | bytes 3076
  23.3 53.5 %copy-start = (bf16[8,512,128]{2,1,0:T(8,128)(2,1)S(1)}, bf16[8,512,128]{2,1,0:T(8,128)(2,1)}, u32[]{:S(2)}) copy-start(bf16[8,512,128]{2,1,0:T(8,128)(2,1)} %param.4) | copy-start | bytes 3145732
  23.4 95.8 %all-to-all-start = ((bf16[8,32,2048]{2,0,1:T(8,128)(2,1)}), bf16[8,32,2048]{2,0,1:T(8,128)(2,1)S(1)}, u32[]{:S(2)}, u32[]{:S(2)}) async-start(bf16[8,32,2048]{2,0,1:T(8,128)(2,1)} %reshape.174), calls=%async_computation | async-start | bytes 2097152 | tf_op jit(solution)/shard_map/all_to_all | solution.py:63
  120.5 5.7 %collective-permute-start = (bf16[9,16,256]{2,0,1:T(8,128)(2,1)S(1)}, bf16[9,16,256]{2,0,1:T(8,128)(2,1)S(1)}, u32[]{:S(2)}, u32[]{:S(2)}) collective-permute-start(bf16[9,16,256]{2,0,1:T(8,128)(2,1)S(1)} %get-tuple-element.19), channel_id=1, source_target_pairs={{0,8},{8,16},{16,24},{1,9},{9,17},{17,25},{2,10},{10,18},{18,26},{... | collective-permute-start | bytes 221192 | tf_op jit(solution)/shard_map/ppermute | solution.py:22
  123.6 6.9 %collective-permute-start.1 = (bf16[9,16,256]{2,0,1:T(8,128)(2,1)S(1)}, bf16[9,16,256]{2,0,1:T(8,128)(2,1)S(1)}, u32[]{:S(2)}, u32[]{:S(2)}) collective-permute-start(bf16[9,16,256]{2,0,1:T(8,128)(2,1)S(1)} %get-tuple-element.20), channel_id=1, source_target_pairs={{8,0},{16,8},{24,16},{9,1},{17,9},{25,17},{10,2},{18,10},{26,18},{... | collective-permute-start | bytes 221192 | tf_op jit(solution)/shard_map/ppermute | solution.py:23
  131.0 14.6 %collective-permute-start.2 = (bf16[146,9,256]{2,0,1:T(8,128)(2,1)S(1)}, bf16[146,9,256]{2,0,1:T(8,128)(2,1)S(1)}, u32[]{:S(2)}, u32[]{:S(2)}) collective-permute-start(bf16[146,9,256]{2,0,1:T(8,128)(2,1)S(1)} %get-tuple-element.17), channel_id=1, source_target_pairs={{0,1},{1,2},{2,3},{3,4},{4,5},{5,6},{6,7},{8,9},{9,10},{10,11},{11... | collective-permute-start | bytes 2018312 | tf_op jit(solution)/shard_map/ppermute | solution.py:22
  137.6 12.4 %collective-permute-start.3 = (bf16[146,9,256]{2,0,1:T(8,128)(2,1)S(1)}, bf16[146,9,256]{2,0,1:T(8,128)(2,1)S(1)}, u32[]{:S(2)}, u32[]{:S(2)}) collective-permute-start(bf16[146,9,256]{2,0,1:T(8,128)(2,1)S(1)} %get-tuple-element.18), channel_id=1, source_target_pairs={{1,0},{2,1},{3,2},{4,3},{5,4},{6,5},{7,6},{9,8},{10,9},{11,10},{12... | collective-permute-start | bytes 2018312 | tf_op jit(solution)/shard_map/ppermute | solution.py:23
where the time goes:
time: 177 us; the launch traced here: 176 us
  blocking collectives  38.9 us (22%)
  between operations  37 us (21%)
  other arithmetic  29.6 us (17%)
  local copies, waits for them, and re-layouts  26 us (15%)
  starting transfers between devices  20.4 us (12%)
  waiting for transfers between devices  14.1 us (8%)
  matrix products  10.3 us (6%)
    unnamed x1, blocking collectives  38.9 us
    another operation x2, local copies, waits for them, and re-layouts, relay(): pieces.reshape(ch_local, n_rows * n_cols, cells)  21.6 us
    another operation x5, other arithmetic, local(): return jnp.stack(results)  15.9 us
    ppermute x2, starting transfers between devices, with_halo(): before = lax.ppermute(last, axis, up)  9.7 us
    ppermute x2, waiting for transfers between devices, with_halo(): after = lax.ppermute(leading, axis, down)  8.65 us
    all_to_all x1, starting transfers between devices, relay(): lax.all_to_all(pieces.reshape(ch_local, n_rows * n_cols, cells), ('ty', '...  6.41 us
    ppermute x2, waiting for transfers between devices, with_halo(): before = lax.ppermute(last, axis, up)  5.4 us
    dot_general x4, matrix products, local(): jnp.einsum('xk,ykc->yxc', col_band, rows_pass, preferred_element_type=jnp...  5.34 us
  transfers between devices with their start and end apart: 5, of which 4 were waited for; matrix products, arithmetic and copies ran while one was open for 8% of the time, Pallas kernels for 0%

commit v1 on v0

--- a/solution.py
+++ b/solution.py
@@ -60,13 +60,20 @@
 
 def relay(pieces):
     ch_local, n_rows, n_cols, cells = pieces.shape
-    arrived = lax.all_to_all(
-        pieces.reshape(ch_local, n_rows * n_cols, cells),
-        ("ty", "tx"),
-        split_axis=1,
-        concat_axis=0,
-        tiled=True,
-    )
+
+    def follow_links_by_axis(x0):
+        field_out = jnp.concatenate(
+            lax.all_to_all(
+                jnp.stack(jnp.split(x0, lax.psum(1, ("ty", "tx")), 1), axis=0),
+                split_axis=0,
+                concat_axis=0,
+                axis_name=("ty", "tx"),
+            ),
+            axis=0,
+        )
+        return field_out
+
+    arrived = follow_links_by_axis(pieces.reshape(ch_local, n_rows * n_cols, cells))
     return arrived.reshape(-1, cells)
 
 

time: 177 us -> 199 us (1.12)
  local copies, waits for them, and re-layouts: 26 us -> 48.1 us
    unnamed x11 -> x42, local copies, waits for them, and re-layouts: 1.68 us -> 21.5 us
    another operation x2 -> x1, local copies, waits for them, and re-layouts: 21.6 us -> 15.1 us  [relay(): pieces.reshape(ch_local, n_rows * n_cols, cells)]
    transpose x0 -> x1, local copies, waits for them, and re-layouts: none -> 5.88 us  [local(): channel_cube.reshape(ch_local, n_rows, TILE_Y, n_cols, TILE_X)]
    split x0 -> x2, local copies, waits for them, and re-layouts: none -> 2.24 us  [follow_links_by_axis(): jnp.split(x0, lax.psum(1, ('ty', 'tx')), 1)]
  transfers between devices with their start and end apart: 5 -> 5, of which waited for: 4 -> 4; matrix products, arithmetic and copies ran while one was open for 8% -> 7% of each run, Pallas kernels for 0% -> 0%
where the time goes in v1:
time: 199 us; the launch traced here: 198 us
  local copies, waits for them, and re-layouts  48.1 us (24%)
  blocking collectives  38.9 us (20%)
  between operations  37 us (19%)
  other arithmetic  29.6 us (15%)
  starting transfers between devices  20.4 us (10%)
  waiting for transfers between devices  14.1 us (7%)
  matrix products  10.3 us (5%)
    unnamed x1, blocking collectives  38.9 us
    unnamed x42, local copies, waits for them, and re-layouts  21.5 us
    another operation x5, other arithmetic, local(): return jnp.stack(results)  15.9 us
    another operation x1, local copies, waits for them, and re-layouts, relay(): pieces.reshape(ch_local, n_rows * n_cols, cells)  15.1 us
    ppermute x2, starting transfers between devices, with_halo(): before = lax.ppermute(last, axis, up)  9.7 us
    ppermute x2, waiting for transfers between devices, with_halo(): after = lax.ppermute(leading, axis, down)  8.65 us
    all_to_all x1, starting transfers between devices, follow_links_by_axis(): lax.all_to_all(jnp.stack(jnp.split(x0, lax.psum(1, ('ty', 'tx')), 1), axi...  6.41 us
    transpose x1, local copies, waits for them, and re-layouts, local(): channel_cube.reshape(ch_local, n_rows, TILE_Y, n_cols, TILE_X)  5.88 us
  transfers between devices with their start and end apart: 5, of which 4 were waited for; matrix products, arithmetic and copies ran while one was open for 7% of the time, Pallas kernels for 0%

profile of v1, /device:TPU:3, one launch (start us, length us, event | category | flops | bytes accessed | tf_op | source)
XLA Modules:
  0.0 198.4 jit_solution(13048434863045019054)
XLA Ops:
  0.0 1.5 copy.807
  1.8 5.9 %copy.808 = bf16[8,4,8,128,16]{4,3,2,1,0:T(8,128)(2,1)} copy(bf16[8,4,8,128,16]{3,1,4,2,0:T(4,128)(2,1)S(1)} %bitcast.153) | data formatting | bytes 2097152 | tf_op jit(solution)/shard_map/transpose | solution.py:94
  7.7 15.1 %reshape_reshape.6 = bf16[8,32,2048]{2,1,0:T(8,128)(2,1)S(1)} reshape(bf16[8,4,8,128,16]{4,3,2,1,0:T(8,128)(2,1)} %copy.808) | data formatting | bytes 2097152 | tf_op jit(solution)/shard_map/reshape;reshape | solution.py:76
  23.7 1.4 fusion.86
  45.5 6.4 %all-to-all-start = ((bf16[32,8,1,2048]{3,1,2,0:T(8,128)(2,1)}), bf16[32,8,1,2048]{3,1,2,0:T(8,128)(2,1)S(1)}, u32[]{:S(2)}, u32[]{:S(2)}) async-start(bf16[32,8,1,2048]{3,1,2,0:T(8,128)(2,1)} %constant_dynamic-update-slice_fusion), calls=%async_computation | async-start | bytes 2097152 | tf_op jit(solution)/shard_map/all_to_all | solution.py:66
  87.9 1.3 multiply_reduce_fusion.4
  91.8 1.2 multiply_reduce_fusion.3
  94.2 1.3 multiply_reduce_fusion.2
  96.8 1.4 multiply_reduce_fusion.1
  99.6 38.9 %all-reduce.4 = f32[256]{0:T(256)S(1)} all-reduce(f32[256]{0:T(256)S(1)} %dynamic-update-slice), channel_id=1, replica_groups=mesh['ty'=4,'tx'=8] {'ty','tx'}, use_global_device_ids=true, to_apply=%add.4 | all-reduce | flops 256 | bytes 2048
  138.5 1.3 convert_convert_fusion
  139.8 1.3 convert_convert_fusion.2
  142.6 3.1 %collective-permute-start = (bf16[9,16,256]{2,0,1:T(8,128)(2,1)S(1)}, bf16[9,16,256]{2,0,1:T(8,128)(2,1)S(1)}, u32[]{:S(2)}, u32[]{:S(2)}) collective-permute-start(bf16[9,16,256]{2,0,1:T(8,128)(2,1)S(1)} %get-tuple-element.19), channel_id=1, source_target_pairs={{0,8},{8,16},{16,24},{1,9},{9,17},{17,25},{2,10},{10,18},{18,26},{... | collective-permute-start | bytes 221192 | tf_op jit(solution)/shard_map/ppermute | solution.py:22
  145.7 2.2 %collective-permute-start.1 = (bf16[9,16,256]{2,0,1:T(8,128)(2,1)S(1)}, bf16[9,16,256]{2,0,1:T(8,128)(2,1)S(1)}, u32[]{:S(2)}, u32[]{:S(2)}) collective-permute-start(bf16[9,16,256]{2,0,1:T(8,128)(2,1)S(1)} %get-tuple-element.20), channel_id=1, source_target_pairs={{8,0},{16,8},{24,16},{9,1},{17,9},{25,17},{10,2},{18,10},{26,18},{... | collective-permute-start | bytes 221192 | tf_op jit(solution)/shard_map/ppermute | solution.py:23
  148.3 4.3 %collective-permute-done.1 = bf16[9,16,256]{2,0,1:T(8,128)(2,1)S(1)} collective-permute-done((bf16[9,16,256]{2,0,1:T(8,128)(2,1)S(1)}, bf16[9,16,256]{2,0,1:T(8,128)(2,1)S(1)}, u32[]{:S(2)}, u32[]{:S(2)}) %collective-permute-start.1) | collective-permute-done | bytes 73760 | tf_op jit(solution)/shard_map/ppermute | solution.py:23
  153.2 6.6 %collective-permute-start.2 = (bf16[146,9,256]{2,0,1:T(8,128)(2,1)S(1)}, bf16[146,9,256]{2,0,1:T(8,128)(2,1)S(1)}, u32[]{:S(2)}, u32[]{:S(2)}) collective-permute-start(bf16[146,9,256]{2,0,1:T(8,128)(2,1)S(1)} %get-tuple-element.17), channel_id=1, source_target_pairs={{0,1},{1,2},{2,3},{3,4},{4,5},{5,6},{6,7},{8,9},{9,10},{10,11},{11... | collective-permute-start | bytes 2018312 | tf_op jit(solution)/shard_map/ppermute | solution.py:22
  159.8 2.1 %collective-permute-start.3 = (bf16[146,9,256]{2,0,1:T(8,128)(2,1)S(1)}, bf16[146,9,256]{2,0,1:T(8,128)(2,1)S(1)}, u32[]{:S(2)}, u32[]{:S(2)}) collective-permute-start(bf16[146,9,256]{2,0,1:T(8,128)(2,1)S(1)} %get-tuple-element.18), channel_id=1, source_target_pairs={{1,0},{2,1},{3,2},{4,3},{5,4},{6,5},{7,6},{9,8},{10,9},{11,10},{12... | collective-permute-start | bytes 2018312 | tf_op jit(solution)/shard_map/ppermute | solution.py:23
  162.8 5.0 %collective-permute-done.2 = bf16[146,9,256]{2,0,1:T(8,128)(2,1)S(1)} collective-permute-done((bf16[146,9,256]{2,0,1:T(8,128)(2,1)S(1)}, bf16[146,9,256]{2,0,1:T(8,128)(2,1)S(1)}, u32[]{:S(2)}, u32[]{:S(2)}) %collective-permute-start.2) | collective-permute-done | bytes 672800 | tf_op jit(solution)/shard_map/ppermute | solution.py:22
  167.8 4.4 %collective-permute-done.3 = bf16[146,9,256]{2,0,1:T(8,128)(2,1)S(1)} collective-permute-done((bf16[146,9,256]{2,0,1:T(8,128)(2,1)S(1)}, bf16[146,9,256]{2,0,1:T(8,128)(2,1)S(1)}, u32[]{:S(2)}, u32[]{:S(2)}) %collective-permute-start.3) | collective-permute-done | bytes 672800 | tf_op jit(solution)/shard_map/ppermute | solution.py:23
  172.2 1.2 convolution_convert_fusion.3
  173.4 1.3 fusion.48
  174.7 1.2 convolution_convert_fusion.2
  176.0 1.3 fusion.51
  177.3 1.2 convolution_convert_fusion.1
  178.5 1.3 fusion.54
  179.9 1.2 convolution_convert_fusion
  181.1 1.3 fusion.57
  182.5 3.2 %fusion.60 = bf16[1,128,16,256]{3,2,1,0:T(8,128)(2,1)S(1)} fusion(f32[256]{0:T(256)S(1)} %get-tuple-element.13, f32[128,16]{1,0:T(8,128)S(1)} %copy.812, f32[]{:T(128)} %bitcast.16, s32[]{:T(128)S(6)} %select_n.301, f32[128,16,256]{2,1,0:T(8,128)S(1)} %fusion.48, pred[]{:T(512)} %bitcast.15, s32[]{:T(128)S(6)} %select_n.298, pred[]{:T(512)} %bitcast.14, ...), kind=kLoop, calls=%fused_computation.90 | loop fusion | flops 6815744 | bytes 3154973 | tf_op jit(solution)/shard_map/stack | solution.py:117
  185.7 3.4 %fusion.61 = bf16[1,128,16,256]{3,2,1,0:T(8,128)(2,1)S(1)} fusion(f32[256]{0:T(256)S(1)} %get-tuple-element.61, f32[128,16]{1,0:T(8,128)S(1)} %copy.812, f32[]{:T(128)} %bitcast.29, s32[]{:T(128)S(6)} %select_n.321, f32[128,16,256]{2,1,0:T(8,128)S(1)} %fusion.51, pred[]{:T(512)} %bitcast.28, s32[]{:T(128)S(6)} %select_n.318, pred[]{:T(512)} %bitcast.27, ...), kind=kLoop, calls=%fused_computation.91 | loop fusion | flops 6815744 | bytes 3154973 | tf_op jit(solution)/shard_map/stack | solution.py:117
  189.1 3.6 %fusion.62 = bf16[1,128,16,256]{3,2,1,0:T(8,128)(2,1)S(1)} fusion(f32[256]{0:T(256)S(1)} %get-tuple-element.62, f32[128,16]{1,0:T(8,128)S(1)} %copy.812, f32[]{:T(128)} %bitcast.42, s32[]{:T(128)S(6)} %select_n.340, f32[128,16,256]{2,1,0:T(8,128)S(1)} %fusion.54, pred[]{:T(512)} %bitcast.41, s32[]{:T(128)S(6)} %select_n.337, pred[]{:T(512)} %bitcast.40, ...), kind=kLoop, calls=%fused_computation.92 | loop fusion | flops 6815744 | bytes 3154973 | tf_op jit(solution)/shard_map/stack | solution.py:117
  192.7 3.4 %fusion.63 = bf16[1,128,16,256]{3,2,1,0:T(8,128)(2,1)S(1)} fusion(f32[256]{0:T(256)S(1)} %get-tuple-element.63, f32[128,16]{1,0:T(8,128)S(1)} %copy.812, f32[]{:T(128)} %bitcast.55, s32[]{:T(128)S(6)} %select_n.359, f32[128,16,256]{2,1,0:T(8,128)S(1)} %fusion.57, pred[]{:T(512)} %bitcast.54, s32[]{:T(128)S(6)} %select_n.356, pred[]{:T(512)} %bitcast.53, ...), kind=kLoop, calls=%fused_computation.93 | loop fusion | flops 6815744 | bytes 3154973 | tf_op jit(solution)/shard_map/stack | solution.py:117
  196.1 2.3 %pad_maximum_fusion = bf16[4,128,16,256]{3,2,1,0:T(8,128)(2,1)} fusion(bf16[1,128,16,256]{3,2,1,0:T(8,128)(2,1)S(1)} %fusion.63, bf16[1,128,16,256]{3,2,1,0:T(8,128)(2,1)S(1)} %fusion.62, bf16[1,128,16,256]{3,2,1,0:T(8,128)(2,1)S(1)} %fusion.61, bf16[1,128,16,256]{3,2,1,0:T(8,128)(2,1)S(1)} %fusion.60), kind=kLoop, calls=%fused_computation.20 | loop fusion | flops 6291456 | bytes 8388608 | tf_op jit(solution)/shard_map/stack | solution.py:117
  (73 shorter events, 30.7 us)
Async XLA Ops:
  32.1 19.8 %copy-start.2 = (s32[4]{0:T(128)S(1)}, s32[4]{0:T(128)}, u32[]{:S(2)}) copy-start(s32[4]{0:T(128)} %param.6) | copy-start | bytes 52
  32.7 22.5 %copy-start.1 = (s32[2,4]{1,0:T(2,128)S(1)}, s32[2,4]{1,0:T(2,128)}, u32[]{:S(2)}) copy-start(s32[2,4]{1,0:T(2,128)} %param.7) | copy-start | bytes 100
  34.6 51.6 %copy-start.3 = (s32[32,8]{0,1:T(8,128)S(1)}, s32[32,8]{0,1:T(8,128)}, u32[]{:S(2)}) copy-start(s32[32,8]{0,1:T(8,128)} %param.5) | copy-start | bytes 3076
  41.7 57.3 %copy-start = (bf16[8,512,128]{2,1,0:T(8,128)(2,1)S(1)}, bf16[8,512,128]{2,1,0:T(8,128)(2,1)}, u32[]{:S(2)}) copy-start(bf16[8,512,128]{2,1,0:T(8,128)(2,1)} %param.4) | copy-start | bytes 3145732
  45.5 95.8 %all-to-all-start = ((bf16[32,8,1,2048]{3,1,2,0:T(8,128)(2,1)}), bf16[32,8,1,2048]{3,1,2,0:T(8,128)(2,1)S(1)}, u32[]{:S(2)}, u32[]{:S(2)}) async-start(bf16[32,8,1,2048]{3,1,2,0:T(8,128)(2,1)} %constant_dynamic-update-slice_fusion), calls=%async_computation | async-start | bytes 2097152 | tf_op jit(solution)/shard_map/all_to_all | solution.py:66
  142.6 5.7 %collective-permute-start = (bf16[9,16,256]{2,0,1:T(8,128)(2,1)S(1)}, bf16[9,16,256]{2,0,1:T(8,128)(2,1)S(1)}, u32[]{:S(2)}, u32[]{:S(2)}) collective-permute-start(bf16[9,16,256]{2,0,1:T(8,128)(2,1)S(1)} %get-tuple-element.19), channel_id=1, source_target_pairs={{0,8},{8,16},{16,24},{1,9},{9,17},{17,25},{2,10},{10,18},{18,26},{... | collective-permute-start | bytes 221192 | tf_op jit(solution)/shard_map/ppermute | solution.py:22
  145.7 6.9 %collective-permute-start.1 = (bf16[9,16,256]{2,0,1:T(8,128)(2,1)S(1)}, bf16[9,16,256]{2,0,1:T(8,128)(2,1)S(1)}, u32[]{:S(2)}, u32[]{:S(2)}) collective-permute-start(bf16[9,16,256]{2,0,1:T(8,128)(2,1)S(1)} %get-tuple-element.20), channel_id=1, source_target_pairs={{8,0},{16,8},{24,16},{9,1},{17,9},{25,17},{10,2},{18,10},{26,18},{... | collective-permute-start | bytes 221192 | tf_op jit(solution)/shard_map/ppermute | solution.py:23
  153.2 14.6 %collective-permute-start.2 = (bf16[146,9,256]{2,0,1:T(8,128)(2,1)S(1)}, bf16[146,9,256]{2,0,1:T(8,128)(2,1)S(1)}, u32[]{:S(2)}, u32[]{:S(2)}) collective-permute-start(bf16[146,9,256]{2,0,1:T(8,128)(2,1)S(1)} %get-tuple-element.17), channel_id=1, source_target_pairs={{0,1},{1,2},{2,3},{3,4},{4,5},{5,6},{6,7},{8,9},{9,10},{10,11},{11... | collective-permute-start | bytes 2018312 | tf_op jit(solution)/shard_map/ppermute | solution.py:22
  159.8 12.4 %collective-permute-start.3 = (bf16[146,9,256]{2,0,1:T(8,128)(2,1)S(1)}, bf16[146,9,256]{2,0,1:T(8,128)(2,1)S(1)}, u32[]{:S(2)}, u32[]{:S(2)}) collective-permute-start(bf16[146,9,256]{2,0,1:T(8,128)(2,1)S(1)} %get-tuple-element.18), channel_id=1, source_target_pairs={{1,0},{2,1},{3,2},{4,3},{5,4},{6,5},{7,6},{9,8},{10,9},{11,10},{12... | collective-permute-start | bytes 2018312 | tf_op jit(solution)/shard_map/ppermute | solution.py:23
